TPU v7x, 128 devices: a whole 4x4x4 slice. The times are simulated.
128 devices in a mesh: row: 8 (over y, z_hi), col: 16 (over x, z_lo, core).
Axes of the slice: x: 4, y: 4, z: 4 (z_hi: 2, z_lo: 2; z = z_hi * 2 + z_lo), core: 2. Of those that a mesh axis runs over, the one named last changes fastest.
Arguments:
- adjacency: bfloat16 [32768, 32768], P('row', 'col'), as said below
- tile_mask: int32 [256, 256], P('row', 'col'), may hold values from 0 to 1, as said below
- out_grad: bfloat16 [32768, 256], P(('row', 'col')), may hold values from -6 to 6
- pre_two: bfloat16 [32768, 256], P(('row', 'col')), may hold values from -6 to 6
- hidden: bfloat16 [32768, 256], P(('col', 'row')), may hold values from -24 to 24
- pre_one: bfloat16 [32768, 256], P(('col', 'row')), may hold values from -6 to 6
- features: bfloat16 [32768, 256], P(('row', 'col')), may hold values from -6 to 6
- w_two: bfloat16 [256, 256], replicated, may hold values from -0.375 to 0.375
- w_one: bfloat16 [256, 256], replicated, may hold values from -0.375 to 0.375
Outputs:
- node_grad: bfloat16 [32768, 256], P(('row', 'col'))
- weight_grad_one: float32 [256, 256], replicated
- weight_grad_two: float32 [256, 256], replicated
Inputs may be any that keep to these rules, and one draw needn't show every extreme that they name: adjacency is symmetric and nonnegative. tile_mask is symmetric and every diagonal tile is 1.
All inputs are finite; a program needn't handle non-finite values.
Results may differ from a plain program's by a relative error of at most 0.02.
Values may be sent and summed in bfloat16 or wider, within the bound.
A program may use at most 128 MiB of HBM per device.

v0:
```python
import jax
import jax.numpy as jnp
from jax import lax
from jax.sharding import PartitionSpec as P


def tile_pick(count, tile_size, tile_total):
    node_ids = lax.broadcasted_iota(jnp.int32, (count, 1), 0)
    tile_ids = lax.broadcasted_iota(jnp.int32, (1, tile_total), 1)
    return (node_ids // tile_size == tile_ids).astype(jnp.bfloat16)


def local(adjacency, tile_mask, out_grad, pre_two, hidden, pre_one, features, w_two, w_one):
    tile_rows, tile_cols = tile_mask.shape
    tile_size = adjacency.shape[0] // tile_rows
    mask_values = tile_mask.astype(jnp.bfloat16)
    shard_nodes = out_grad.shape[0]
    weight_scale = 4.0 * shard_nodes ** (-0.5)
    contract_rows = (((0,), (0,)), ((), ()))
    contract_cols = (((1,), (1,)), ((), ()))
    grad_two = jnp.where(pre_two > 0, out_grad, jnp.zeros_like(out_grad))
    shard_rows = lax.all_gather(grad_two, "col", axis=0, tiled=True)
    count = shard_rows.shape[0]
    strip_rows = adjacency
    picker = tile_pick(count, tile_size, tile_rows)
    strip_mask = jnp.dot(picker, mask_values, preferred_element_type=jnp.float32).astype(
        jnp.bfloat16
    )
    strip_rows = (strip_rows.reshape(count, tile_cols, tile_size) * strip_mask[:, :, None]).reshape(
        count, adjacency.shape[1]
    )
    column_part = lax.dot_general(
        strip_rows, shard_rows, contract_rows, preferred_element_type=jnp.float32
    )
    column_part = column_part.astype(jnp.bfloat16).astype(jnp.float32)
    prop_two = lax.psum_scatter(
        column_part.astype(jnp.bfloat16), "row", scatter_dimension=0, tiled=True
    )
    back_grad = lax.dot_general(prop_two, w_two, contract_cols, preferred_element_type=jnp.float32)
    grad_one = jnp.where(pre_one > 0, back_grad, jnp.zeros_like(back_grad)).astype(jnp.bfloat16)
    shard_rows = lax.all_gather(grad_one, "row", axis=0, tiled=True)
    count = shard_rows.shape[0]
    strip_cols = adjacency
    picker = tile_pick(count, tile_size, tile_cols)
    strip_mask = lax.dot_general(
        mask_values, picker, contract_cols, preferred_element_type=jnp.float32
    ).astype(jnp.bfloat16)
    strip_cols = (strip_cols.reshape(tile_rows, tile_size, count) * strip_mask[:, None, :]).reshape(
        adjacency.shape[0], count
    )
    row_part = jnp.dot(strip_cols, shard_rows, preferred_element_type=jnp.float32)
    term_two = lax.dot_general(hidden, prop_two, contract_rows, preferred_element_type=jnp.float32)
    summed_two = lax.psum(term_two, ("row", "col"))
    row_part = row_part.astype(jnp.bfloat16).astype(jnp.float32)
    prop_one = lax.psum_scatter(
        row_part.astype(jnp.bfloat16), "col", scatter_dimension=0, tiled=True
    )
    term_one = lax.dot_general(
        features, prop_one, contract_rows, preferred_element_type=jnp.float32
    )
    node_grad = lax.dot_general(
        prop_one, w_one, contract_cols, preferred_element_type=jnp.float32
    ).astype(jnp.bfloat16)
    summed_one = lax.psum(term_one, ("row", "col"))
    return (node_grad, summed_one * weight_scale, summed_two * weight_scale)


def solution(mesh):
    return jax.shard_map(
        local,
        mesh=mesh,
        in_specs=(
            P("row", "col"),
            P("row", "col"),
            P(("row", "col"), None),
            P(("row", "col"), None),
            P(("col", "row"), None),
            P(("col", "row"), None),
            P(("row", "col"), None),
            P(),
            P(),
        ),
        out_specs=(P(("row", "col"), None), P(), P()),
        check_vma=False,
    )
```

profile of v0, /device:TPU:1, one launch (start us, length us, event | category | flops | bytes accessed | tf_op | source)
XLA Modules:
  0.0 437.8 jit_solution(10373811274106707431)
XLA Ops:
  7.2 0.0 copy-start
  7.2 0.0 all-gather.3.cloned.1.call-start
  7.2 1.7 compare_select_fusion
  8.9 0.0 all-gather.3.cloned.1.call-update
  8.9 0.0 reduce-scatter.3.cloned.1.call-start
  9.0 0.9 convolution_convert_fusion.1
  9.9 0.5 copy.15
  10.4 37.4 %all-gather.3.cloned.1.call-done = bf16[4096,256]{1,0:T(8,128)(2,1)} async-done(((bf16[256,256]{1,0:T(8,128)(2,1)}), bf16[4096,256]{1,0:T(8,128)(2,1)}) %all-gather.3.cloned.1.call-update) | async-done | bytes 2097168 | tf_op jit(solution)/shard_map/all_gather | solution.py:22
  47.7 18.8 %mul.31 = bf16[4096,16,128]{2,1,0:T(8,128)(2,1)} broadcast(bf16[4096,16]{1,0:T(8,128)(2,1)S(1)} %copy.15), dimensions={0,1} | broadcast | bytes 16908288 | tf_op jit(solution)/shard_map/mul | solution.py:29
  66.5 0.0 copy-done.7
  66.5 14.3 %fusion.2 = bf16[2048,256]{1,0:T(8,128)(2,1)} fusion(bf16[4096,256]{1,0:T(8,128)(2,1)S(1)} %copy-done.7, bf16[4096,2048]{1,0:T(8,128)(2,1)} %param.9, bf16[512,8,16,128]{3,2,1,0:T(8,128)(2,1)} %bitcast.25), kind=kOutput, calls=%fused_computation.6 | convolution fusion | flops 4303880192 | bytes 36700160 | tf_op jit(solution)/shard_map/dot_general | solution.py:32
  80.9 0.0 reduce-scatter.3.cloned.1.call-update
  80.9 0.0 all-gather.5.cloned.1.call-start
  80.9 70.7 %reduce-scatter.3.cloned.1.call-done = bf16[256,256]{1,0:T(8,128)(2,1)} async-done(((bf16[2048,256]{1,0:T(8,128)(2,1)}), bf16[256,256]{1,0:T(8,128)(2,1)}) %reduce-scatter.3.cloned.1.call-update) | async-done | bytes 131088 | tf_op jit(solution)/shard_map/reduce_scatter | solution.py:36
  151.6 1.8 fusion.4
  153.4 0.0 all-gather.5.cloned.1.call-update
  153.4 0.0 reduce-scatter.5.cloned.1.call-start
  153.5 0.5 fusion.3
  154.0 13.9 %bitcast_multiply_fusion.2 = bf16[4096,2048]{1,0:T(8,128)(2,1)} fusion(bf16[4096,2048]{1,0:T(8,128)(2,1)} %param.9, bf16[32,2048]{1,0:T(8,128)(2,1)S(1)} %fusion.3), kind=kLoop, calls=%fused_computation.3 | loop fusion | flops 8388608 | bytes 33685504 | tf_op jit(solution)/shard_map/mul | solution.py:48
  167.9 33.0 %all-gather.5.cloned.1.call-done = bf16[2048,256]{1,0:T(8,128)(2,1)} async-done(((bf16[256,256]{1,0:T(8,128)(2,1)}), bf16[2048,256]{1,0:T(8,128)(2,1)}) %all-gather.5.cloned.1.call-update) | async-done | bytes 1048592 | tf_op jit(solution)/shard_map/all_gather | solution.py:41
  201.0 11.9 %convolution_convert_fusion = bf16[4096,256]{1,0:T(8,128)(2,1)} fusion(bf16[4096,2048]{1,0:T(8,128)(2,1)} %bitcast_multiply_fusion.2, bf16[2048,256]{1,0:T(8,128)(2,1)} %all-gather.5.cloned.1.call-done), kind=kOutput, calls=%fused_computation.4 | convolution fusion | flops 4296015872 | bytes 19922944 | tf_op jit(solution)/shard_map/dot_general | solution.py:51
  212.9 0.0 reduce-scatter.5.cloned.1.call-update
  212.9 0.0 all-reduce.3.cloned.1.call-start
  213.0 0.9 convolution_bitcast_fusion
  213.9 60.4 %reduce-scatter.5.cloned.1.call-done = bf16[256,256]{1,0:T(8,128)(2,1)} async-done(((bf16[4096,256]{1,0:T(8,128)(2,1)}), bf16[256,256]{1,0:T(8,128)(2,1)}) %reduce-scatter.5.cloned.1.call-update) | async-done | bytes 131088 | tf_op jit(solution)/shard_map/reduce_scatter | solution.py:55
  274.3 1.8 convolution_bitcast_fusion.1
  276.2 0.0 all-reduce.3.cloned.1.call-update
  276.2 1.8 convolution_convert_fusion.3
  278.0 150.5 %all-reduce.3.cloned.1.call-done = (f32[256,256]{0,1:T(8,128)}, f32[256,256]{0,1:T(8,128)}) async-done(((f32[256,256]{0,1:T(8,128)}, f32[256,256]{0,1:T(8,128)}), (f32[256,256]{0,1:T(8,128)}, f32[256,256]{0,1:T(8,128)})) %all-reduce.3.cloned.1.call-update) | async-done | bytes 524304 | tf_op jit(solution)/shard_map/psum | solution.py:64
  428.5 1.1 broadcast_multiply_fusion
  429.6 0.8 copy.16
  430.4 0.8 copy.17
  (16 shorter events, 0.0 us)
Async XLA Ops:
  7.2 144.5 %copy-start = (bf16[256,256]{1,0:T(8,128)(2,1)S(1)}, bf16[256,256]{1,0:T(8,128)(2,1)}, u32[]{:S(2)}) copy-start(bf16[256,256]{1,0:T(8,128)(2,1)} %param.16) | copy-start | bytes 393220
  7.2 40.5 %all-gather.3.cloned.1.call-start = ((), (), s32[]{:S(2)}) async-start(), calls=%async_computation.2 | async-start | bytes 2228224 | tf_op jit(solution)/shard_map/all_gather | solution.py:22
  8.9 142.7 %reduce-scatter.3.cloned.1.call-start = ((), (), s32[]{:S(2)}) async-start(), calls=%async_computation.3 | async-start | bytes 1179648 | tf_op jit(solution)/shard_map/reduce_scatter | solution.py:36
  47.7 18.8 %copy-start.7 = (bf16[4096,256]{1,0:T(8,128)(2,1)S(1)}, bf16[4096,256]{1,0:T(8,128)(2,1)}, u32[]{:S(2)}) copy-start(bf16[4096,256]{1,0:T(8,128)(2,1)} %all-gather.3.cloned.1.call-done) | copy-start | bytes 6291460
  66.5 85.1 %copy-start.3 = (bf16[256,256]{1,0:T(8,128)(2,1)S(1)}, bf16[256,256]{1,0:T(8,128)(2,1)}, u32[]{:S(2)}) copy-start(bf16[256,256]{1,0:T(8,128)(2,1)} %param.14) | copy-start | bytes 393220
  66.5 87.0 %copy-start.6 = (s32[32,16]{0,1:T(8,128)S(1)}, s32[32,16]{0,1:T(8,128)}, u32[]{:S(2)}) copy-start(s32[32,16]{0,1:T(8,128)} %param.10) | copy-start | bytes 6148
  80.9 120.1 %all-gather.5.cloned.1.call-start = ((), (), s32[]{:S(2)}) async-start(), calls=%async_computation.4 | async-start | bytes 1179648 | tf_op jit(solution)/shard_map/all_gather | solution.py:41
  153.4 120.9 %reduce-scatter.5.cloned.1.call-start = ((), (), s32[]{:S(2)}) async-start(), calls=%async_computation.5 | async-start | bytes 2228224 | tf_op jit(solution)/shard_map/reduce_scatter | solution.py:55
  167.9 45.0 %copy-start.1 = (bf16[256,256]{1,0:T(8,128)(2,1)S(1)}, bf16[256,256]{1,0:T(8,128)(2,1)}, u32[]{:S(2)}) copy-start(bf16[256,256]{1,0:T(8,128)(2,1)} %reduce-scatter.3.cloned.1.call-done) | copy-start | bytes 393220
  167.9 45.0 %copy-start.4 = (bf16[256,256]{1,0:T(8,128)(2,1)S(1)}, bf16[256,256]{1,0:T(8,128)(2,1)}, u32[]{:S(2)}) copy-start(bf16[256,256]{1,0:T(8,128)(2,1)} %param.13) | copy-start | bytes 393220
  167.9 106.4 %copy-start.5 = (bf16[256,256]{1,0:T(8,128)(2,1)S(1)}, bf16[256,256]{1,0:T(8,128)(2,1)}, u32[]{:S(2)}) copy-start(bf16[256,256]{1,0:T(8,128)(2,1)} %param.15) | copy-start | bytes 393220
  167.9 108.2 %copy-start.2 = (bf16[256,256]{1,0:T(8,128)(2,1)S(1)}, bf16[256,256]{1,0:T(8,128)(2,1)}, u32[]{:S(2)}) copy-start(bf16[256,256]{1,0:T(8,128)(2,1)} %param.17) | copy-start | bytes 393220
  212.9 215.6 %all-reduce.3.cloned.1.call-start = ((), (), s32[]{:S(2)}) async-start(), calls=%async_computation.6 | async-start | bytes 1048576 | tf_op jit(solution)/shard_map/psum | solution.py:64
Sparse Core Ops, SparseCore 0:
  10.3 37.4 all-gather.2
  81.0 70.5 reduce-scatter.2
  154.5 46.3 all-gather.4
  213.0 61.2 reduce-scatter.4
  279.7 148.7 all-reduce.2
where the time goes:
time: 438 us
  waiting for transfers between devices  352 us (80%)
  matrix products  33.9 us (8%)
  local copies, waits for them, and re-layouts  21 us (5%)
  other arithmetic  16.7 us (4%)
  between operations  13.9 us (3%)
    psum x1, waiting for transfers between devices, local(): summed_one = lax.psum(term_one, ('row', 'col'))  151 us
    reduce_scatter x1, waiting for transfers between devices, local(): lax.psum_scatter(column_part.astype(jnp.bfloat16), 'row', scatter_dimensi...  70.7 us
    reduce_scatter x1, waiting for transfers between devices, local(): lax.psum_scatter(row_part.astype(jnp.bfloat16), 'col', scatter_dimension=...  60.4 us
    all_gather x1, waiting for transfers between devices, local(): shard_rows = lax.all_gather(grad_two, 'col', axis=0, tiled=True)  37.4 us
    all_gather x1, waiting for transfers between devices, local(): shard_rows = lax.all_gather(grad_one, 'row', axis=0, tiled=True)  33 us
    mul x1, local copies, waits for them, and re-layouts, local(): strip_rows.reshape(count, tile_cols, tile_size) * strip_mask[:, :, None]  18.8 us
    dot_general x1, matrix products, local(): lax.dot_general(strip_rows, shard_rows, contract_rows, preferred_element_...  14.3 us
    mul x1, other arithmetic, local(): strip_cols.reshape(tile_rows, tile_size, count) * strip_mask[:, None, :]  13.9 us
  transfers between devices with their start and end apart: 5, of which 5 were waited for; matrix products, arithmetic and copies ran while one was open for 4% of the time, Pallas kernels for 0%

commit v1 on v0

--- a/solution.py
+++ b/solution.py
@@ -61,7 +61,7 @@
     node_grad = lax.dot_general(
         prop_one, w_one, contract_cols, preferred_element_type=jnp.float32
     ).astype(jnp.bfloat16)
-    summed_one = lax.psum(term_one, ("row", "col"))
+    summed_one = lax.psum(lax.psum(term_one, "col"), "row")
     return (node_grad, summed_one * weight_scale, summed_two * weight_scale)
 
 

time: 438 us -> 640 us (1.46)
  waiting for transfers between devices: 352 us -> 548 us
    psum x1 -> x3, waiting for transfers between devices: 151 us -> 345 us  [the longest x2 196 us: local(): summed_one = lax.psum(lax.psum(term_one, 'col'), 'row')]
  transfers between devices with their start and end apart: 5 -> 7, of which waited for: 5 -> 7; matrix products, arithmetic and copies ran while one was open for 4% -> 3% of each run, Pallas kernels for 0% -> 0%
where the time goes in v1:
time: 640 us; the launch traced here: 634 us
  waiting for transfers between devices  548 us (86%)
  matrix products  33.9 us (5%)
  local copies, waits for them, and re-layouts  21 us (3%)
  other arithmetic  17.5 us (3%)
  between operations  14.2 us (2%)
    psum x2, waiting for transfers between devices, local(): summed_one = lax.psum(lax.psum(term_one, 'col'), 'row')  196 us
    psum x1, waiting for transfers between devices, local(): summed_two = lax.psum(term_two, ('row', 'col'))  149 us
    reduce_scatter x1, waiting for transfers between devices, local(): lax.psum_scatter(column_part.astype(jnp.bfloat16), 'row', scatter_dimensi...  70.6 us
    reduce_scatter x1, waiting for transfers between devices, local(): lax.psum_scatter(row_part.astype(jnp.bfloat16), 'col', scatter_dimension=...  61.5 us
    all_gather x1, waiting for transfers between devices, local(): shard_rows = lax.all_gather(grad_two, 'col', axis=0, tiled=True)  37.4 us
    all_gather x1, waiting for transfers between devices, local(): shard_rows = lax.all_gather(grad_one, 'row', axis=0, tiled=True)  33 us
    mul x1, local copies, waits for them, and re-layouts, local(): strip_rows.reshape(count, tile_cols, tile_size) * strip_mask[:, :, None]  18.8 us
    dot_general x1, matrix products, local(): lax.dot_general(strip_rows, shard_rows, contract_rows, preferred_element_...  14.3 us
  transfers between devices with their start and end apart: 7, of which 7 were waited for; matrix products, arithmetic and copies ran while one was open for 3% of the time, Pallas kernels for 0%

profile of v1, /device:TPU:1, one launch (start us, length us, event | category | flops | bytes accessed | tf_op | source)
XLA Modules:
  0.0 634.4 jit_solution(17752263189853147945)
XLA Ops:
  7.2 0.0 all-gather.3.cloned.1.call-start
  7.2 1.7 compare_select_fusion
  8.9 0.0 reduce-scatter.3.cloned.1.call-start
  9.0 0.9 convolution_convert_fusion.1
  9.9 0.5 copy.15
  10.4 37.4 %all-gather.3.cloned.1.call-done = bf16[4096,256]{1,0:T(8,128)(2,1)} async-done(((bf16[256,256]{1,0:T(8,128)(2,1)}), bf16[4096,256]{1,0:T(8,128)(2,1)}) %all-gather.3.cloned.1.call-update) | async-done | bytes 2097168 | tf_op jit(solution)/shard_map/all_gather | solution.py:22
  47.7 18.8 %mul.31 = bf16[4096,16,128]{2,1,0:T(8,128)(2,1)} broadcast(bf16[4096,16]{1,0:T(8,128)(2,1)S(1)} %copy.15), dimensions={0,1} | broadcast | bytes 16908288 | tf_op jit(solution)/shard_map/mul | solution.py:29
  66.5 14.3 %fusion.2 = bf16[2048,256]{1,0:T(8,128)(2,1)} fusion(bf16[4096,256]{1,0:T(8,128)(2,1)S(1)} %copy-done.7, bf16[4096,2048]{1,0:T(8,128)(2,1)} %param.9, bf16[512,8,16,128]{3,2,1,0:T(8,128)(2,1)} %bitcast.25), kind=kOutput, calls=%fused_computation.6 | convolution fusion | flops 4303880192 | bytes 36700160 | tf_op jit(solution)/shard_map/dot_general | solution.py:32
  80.8 0.0 all-gather.5.cloned.1.call-start
  80.9 70.6 %reduce-scatter.3.cloned.1.call-done = bf16[256,256]{1,0:T(8,128)(2,1)} async-done(((bf16[2048,256]{1,0:T(8,128)(2,1)}), bf16[256,256]{1,0:T(8,128)(2,1)}) %reduce-scatter.3.cloned.1.call-update) | async-done | bytes 131088 | tf_op jit(solution)/shard_map/reduce_scatter | solution.py:36
  151.6 1.8 fusion.4
  153.3 0.0 all-gather.5.cloned.1.call-update
  153.4 0.0 reduce-scatter.5.cloned.1.call-start
  153.4 0.5 fusion.3
  153.9 13.9 %bitcast_multiply_fusion.2 = bf16[4096,2048]{1,0:T(8,128)(2,1)} fusion(bf16[4096,2048]{1,0:T(8,128)(2,1)} %param.9, bf16[32,2048]{1,0:T(8,128)(2,1)S(1)} %fusion.3), kind=kLoop, calls=%fused_computation.3 | loop fusion | flops 8388608 | bytes 33685504 | tf_op jit(solution)/shard_map/mul | solution.py:48
  167.9 33.0 %all-gather.5.cloned.1.call-done = bf16[2048,256]{1,0:T(8,128)(2,1)} async-done(((bf16[256,256]{1,0:T(8,128)(2,1)}), bf16[2048,256]{1,0:T(8,128)(2,1)}) %all-gather.5.cloned.1.call-update) | async-done | bytes 1048592 | tf_op jit(solution)/shard_map/all_gather | solution.py:41
  200.9 11.9 %convolution_convert_fusion = bf16[4096,256]{1,0:T(8,128)(2,1)} fusion(bf16[4096,2048]{1,0:T(8,128)(2,1)} %bitcast_multiply_fusion.2, bf16[2048,256]{1,0:T(8,128)(2,1)} %all-gather.5.cloned.1.call-done), kind=kOutput, calls=%fused_computation.4 | convolution fusion | flops 4296015872 | bytes 19922944 | tf_op jit(solution)/shard_map/dot_general | solution.py:51
  212.8 0.0 all-reduce.4.cloned.1.call-start
  212.8 61.5 %reduce-scatter.5.cloned.1.call-done = bf16[256,256]{1,0:T(8,128)(2,1)} async-done(((bf16[4096,256]{1,0:T(8,128)(2,1)}), bf16[256,256]{1,0:T(8,128)(2,1)}) %reduce-scatter.5.cloned.1.call-update) | async-done | bytes 131088 | tf_op jit(solution)/shard_map/reduce_scatter | solution.py:55
  274.4 1.8 convolution_bitcast_fusion.1
  276.2 0.0 all-reduce.8.cloned.1.call-start
  276.3 0.9 convolution_bitcast_fusion
  277.2 0.0 all-reduce.8.cloned.1.call-update
  277.3 0.0 all-reduce.6.cloned.1.call-start
  277.3 119.8 %all-reduce.4.cloned.1.call-done = f32[256,256]{0,1:T(8,128)} async-done(((f32[256,256]{0,1:T(8,128)}), f32[256,256]{0,1:T(8,128)}) %all-reduce.4.cloned.1.call-update) | async-done | bytes 262160 | tf_op jit(solution)/shard_map/psum | solution.py:64
  397.1 149.3 %all-reduce.8.cloned.1.call-done = f32[256,256]{0,1:T(8,128)} async-done(((f32[256,256]{0,1:T(8,128)}), f32[256,256]{0,1:T(8,128)}) %all-reduce.8.cloned.1.call-update) | async-done | bytes 262160 | tf_op jit(solution)/shard_map/psum | solution.py:53
  546.4 1.0 broadcast_multiply_fusion
  547.4 0.8 copy.17
  548.2 1.8 convolution_convert_fusion.3
  550.0 75.8 %all-reduce.6.cloned.1.call-done = f32[256,256]{0,1:T(8,128)} async-done(((f32[256,256]{0,1:T(8,128)}), f32[256,256]{0,1:T(8,128)}) %all-reduce.6.cloned.1.call-update) | async-done | bytes 262160 | tf_op jit(solution)/shard_map/psum | solution.py:64
  625.8 1.0 broadcast_multiply_fusion.1
  626.8 0.8 copy.16
  (23 shorter events, 0.1 us)
Async XLA Ops:
  7.2 144.4 %copy-start = (bf16[256,256]{1,0:T(8,128)(2,1)S(1)}, bf16[256,256]{1,0:T(8,128)(2,1)}, u32[]{:S(2)}) copy-start(bf16[256,256]{1,0:T(8,128)(2,1)} %param.16) | copy-start | bytes 393220
  7.2 40.5 %all-gather.3.cloned.1.call-start = ((), (), s32[]{:S(2)}) async-start(), calls=%async_computation.2 | async-start | bytes 2228224 | tf_op jit(solution)/shard_map/all_gather | solution.py:22
  8.9 142.6 %reduce-scatter.3.cloned.1.call-start = ((), (), s32[]{:S(2)}) async-start(), calls=%async_computation.3 | async-start | bytes 1179648 | tf_op jit(solution)/shard_map/reduce_scatter | solution.py:36
  47.7 18.8 %copy-start.7 = (bf16[4096,256]{1,0:T(8,128)(2,1)S(1)}, bf16[4096,256]{1,0:T(8,128)(2,1)}, u32[]{:S(2)}) copy-start(bf16[4096,256]{1,0:T(8,128)(2,1)} %all-gather.3.cloned.1.call-done) | copy-start | bytes 6291460
  66.5 85.0 %copy-start.3 = (bf16[256,256]{1,0:T(8,128)(2,1)S(1)}, bf16[256,256]{1,0:T(8,128)(2,1)}, u32[]{:S(2)}) copy-start(bf16[256,256]{1,0:T(8,128)(2,1)} %param.14) | copy-start | bytes 393220
  66.5 86.9 %copy-start.6 = (s32[32,16]{0,1:T(8,128)S(1)}, s32[32,16]{0,1:T(8,128)}, u32[]{:S(2)}) copy-start(s32[32,16]{0,1:T(8,128)} %param.10) | copy-start | bytes 6148
  80.8 120.1 %all-gather.5.cloned.1.call-start = ((), (), s32[]{:S(2)}) async-start(), calls=%async_computation.4 | async-start | bytes 1179648 | tf_op jit(solution)/shard_map/all_gather | solution.py:41
  153.4 121.0 %reduce-scatter.5.cloned.1.call-start = ((), (), s32[]{:S(2)}) async-start(), calls=%async_computation.5 | async-start | bytes 2228224 | tf_op jit(solution)/shard_map/reduce_scatter | solution.py:55
  167.9 106.5 %copy-start.4 = (bf16[256,256]{1,0:T(8,128)(2,1)S(1)}, bf16[256,256]{1,0:T(8,128)(2,1)}, u32[]{:S(2)}) copy-start(bf16[256,256]{1,0:T(8,128)(2,1)} %param.15) | copy-start | bytes 393220
  167.9 108.4 %copy-start.1 = (bf16[256,256]{1,0:T(8,128)(2,1)S(1)}, bf16[256,256]{1,0:T(8,128)(2,1)}, u32[]{:S(2)}) copy-start(bf16[256,256]{1,0:T(8,128)(2,1)} %reduce-scatter.3.cloned.1.call-done) | copy-start | bytes 393220
  167.9 108.4 %copy-start.5 = (bf16[256,256]{1,0:T(8,128)(2,1)S(1)}, bf16[256,256]{1,0:T(8,128)(2,1)}, u32[]{:S(2)}) copy-start(bf16[256,256]{1,0:T(8,128)(2,1)} %param.13) | copy-start | bytes 393220
  167.9 380.3 %copy-start.2 = (bf16[256,256]{1,0:T(8,128)(2,1)S(1)}, bf16[256,256]{1,0:T(8,128)(2,1)}, u32[]{:S(2)}) copy-start(bf16[256,256]{1,0:T(8,128)(2,1)} %param.17) | copy-start | bytes 393220
  212.8 184.3 %all-reduce.4.cloned.1.call-start = ((), (), s32[]{:S(2)}) async-start(), calls=%async_computation.6 | async-start | bytes 524288 | tf_op jit(solution)/shard_map/psum | solution.py:64
  276.2 270.2 %all-reduce.8.cloned.1.call-start = ((), (), s32[]{:S(2)}) async-start(), calls=%async_computation.8 | async-start | bytes 524288 | tf_op jit(solution)/shard_map/psum | solution.py:53
  277.3 348.5 %all-reduce.6.cloned.1.call-start = ((), (), s32[]{:S(2)}) async-start(), calls=%async_computation.7 | async-start | bytes 524288 | tf_op jit(solution)/shard_map/psum | solution.py:64
Sparse Core Ops, SparseCore 0:
  10.3 37.4 all-gather.2
  81.0 70.5 reduce-scatter.2
  154.5 46.3 all-gather.4
  212.9 61.4 reduce-scatter.4
  277.3 119.7 all-reduce.3
  402.3 144.0 all-reduce.7
  548.9 76.8 all-reduce.5
